TPU v7x, 32 devices: a whole 2x2x4 slice. The times are simulated.
32 devices in a mesh: shard: 4 (over y, x), ctx: 8 (over z, core).
Axes of the slice: x: 2, y: 2, z: 4, core: 2. Of those that a mesh axis runs over, the one named last changes fastest.
Arguments:
- tokens: bfloat16 [4, 1024, 768], P('shard', 'ctx'), may hold values from -60 to 60
- lengths: int32 [4], P('shard'), may hold values from 128 to 1024, as said below
- cotangent: bfloat16 [4, 1024, 768], P('shard', 'ctx'), may hold values from -6 to 6
- w_qkv: bfloat16 [768, 2304], P('shard'), may hold values from -0.21875 to 0.21875
- b_query: bfloat16 [768], P('shard'), may hold values from -3 to 3
- b_value: bfloat16 [768], P('shard'), may hold values from -3 to 3
- w_out: bfloat16 [768, 768], P('shard'), may hold values from -3.5 to 3.5
- b_out: bfloat16 [768], P('shard'), may hold values from -3 to 3
- ln1_gain: bfloat16 [768], P('shard'), may hold values from 0.25 to 1.75
- ln1_bias: bfloat16 [768], P('shard'), may hold values from -3 to 3
- w_up: bfloat16 [768, 3072], P('shard'), may hold values from -0.21875 to 0.21875
- b_up: bfloat16 [3072], P('shard'), may hold values from -3 to 3
- w_down: bfloat16 [3072, 768], P('shard'), may hold values from -0.109375 to 0.109375
- b_down: bfloat16 [768], P('shard'), may hold values from -3 to 3
- ln2_gain: bfloat16 [768], P('shard'), may hold values from 0.25 to 1.75
- ln2_bias: bfloat16 [768], P('shard'), may hold values from -3 to 3
Outputs:
- output: bfloat16 [4, 1024, 768], P('shard', 'ctx')
- tokens_grad: float32 [4, 1024, 768], P('shard', 'ctx')
- w_qkv_grad: float32 [768, 2304], P('shard')
- b_query_grad: float32 [768], P('shard')
- b_value_grad: float32 [768], P('shard')
- w_out_grad: float32 [768, 768], P('shard')
- b_out_grad: float32 [768], P('shard')
- ln1_gain_grad: float32 [768], P('shard')
- ln1_bias_grad: float32 [768], P('shard')
- w_up_grad: float32 [768, 3072], P('shard')
- b_up_grad: float32 [3072], P('shard')
- w_down_grad: float32 [3072, 768], P('shard')
- b_down_grad: float32 [768], P('shard')
- ln2_gain_grad: float32 [768], P('shard')
- ln2_bias_grad: float32 [768], P('shard')
Inputs may be any that keep to these rules, and one draw needn't show every extreme that they name: `lengths`: each sequence has at least one valid token; some sequence is entirely valid.
All inputs are finite; a program needn't handle non-finite values.
Results may differ from a plain program's by a relative error of at most 0.035.
The roundings to bfloat16 on the way count: a program that leaves them out, or rounds other values in their place, can miss the bound.
Values may be sent and summed in bfloat16 or wider, within the bound.
A program may use at most 128 MiB of HBM per device.

v0:
```python
import math
import jax
import jax.numpy as jnp
from jax import lax
from jax.sharding import PartitionSpec as P

HEADS = 12
EPS = 1e-06


def normalize(z):
    centre = z - jnp.mean(z, axis=-1, keepdims=True)
    rstd = lax.rsqrt(jnp.mean(centre * centre, axis=-1, keepdims=True) + EPS)
    return (centre * rstd, rstd)


def norm_back(dnorm, normed, rstd):
    return rstd * (
        dnorm
        - jnp.mean(dnorm, axis=-1, keepdims=True)
        - normed * jnp.mean(dnorm * normed, axis=-1, keepdims=True)
    )


def gelu_exact(t):
    return jax.nn.gelu(t, approximate=False)


def contract_dims(left, right, left_dim, right_dim):
    return lax.dot_general(
        left, right, (((left_dim,), (right_dim,)), ((), ())), preferred_element_type=jnp.float32
    )


def heads_first(a):
    return a.reshape(HEADS, a.shape[0] // HEADS, a.shape[1])


def local(
    tokens,
    lengths,
    cotangent,
    w_qkv,
    b_query,
    b_value,
    w_out,
    b_out,
    ln1_gain,
    ln1_bias,
    w_up,
    b_up,
    w_down,
    b_down,
    ln2_gain,
    ln2_bias,
):
    single_float = jnp.float32
    bf16 = jnp.bfloat16
    full = (
        lax.all_gather(w_qkv, "shard", axis=0, tiled=True),
        lax.all_gather(b_query, "shard", axis=0, tiled=True),
        lax.all_gather(b_value, "shard", axis=0, tiled=True),
        lax.all_gather(w_out, "shard", axis=0, tiled=True),
        lax.all_gather(b_out, "shard", axis=0, tiled=True),
        lax.all_gather(ln1_gain, "shard", axis=0, tiled=True),
        lax.all_gather(ln1_bias, "shard", axis=0, tiled=True),
        lax.all_gather(w_up, "shard", axis=0, tiled=True),
        lax.all_gather(b_up, "shard", axis=0, tiled=True),
        lax.all_gather(w_down, "shard", axis=0, tiled=True),
        lax.all_gather(b_down, "shard", axis=0, tiled=True),
        lax.all_gather(ln2_gain, "shard", axis=0, tiled=True),
        lax.all_gather(ln2_bias, "shard", axis=0, tiled=True),
    )
    wq_full, wo_full, wu_full, wd_full = (full[0], full[3], full[7], full[9])
    bq, bv, bo = (
        full[1].astype(single_float),
        full[2].astype(single_float),
        full[4].astype(single_float),
    )
    g1, c1, bu = (
        full[5].astype(single_float),
        full[6].astype(single_float),
        full[8].astype(single_float),
    )
    bd, g2, c2 = (
        full[10].astype(single_float),
        full[11].astype(single_float),
        full[12].astype(single_float),
    )
    x = tokens[0]
    width = x.shape[1]
    head_size = width // HEADS
    scale = 1.0 / math.sqrt(head_size)
    limit = lengths[0]
    qkv_t = contract_dims(wq_full, x, 0, 1)
    query_t = (qkv_t[:width] + bq[:, None]).astype(bf16)
    keys_t = qkv_t[width : 2 * width].astype(bf16)
    values_t = (qkv_t[2 * width :] + bv[:, None]).astype(bf16)
    all_keys, all_values = (
        lax.all_gather(keys_t, "ctx", axis=1, tiled=True),
        lax.all_gather(values_t, "ctx", axis=1, tiled=True),
    )
    total = all_keys.shape[1]
    valid = jnp.arange(total, dtype=jnp.int32) < limit

    def head_fwd(operations):
        query_index, key_index, value_index = operations
        scores = contract_dims(query_index, key_index, 0, 0) * scale
        scores = jnp.where(valid[None, :], scores, -1e30)
        peak = jnp.max(scores, axis=1, keepdims=True)
        lse = peak + jnp.log(jnp.sum(jnp.exp(scores - peak), axis=1, keepdims=True))
        probs = jnp.exp(scores - lse).astype(bf16)
        return (contract_dims(value_index, probs, 1, 1), lse[:, 0])

    ctx_heads, lse_all = lax.map(
        head_fwd, (heads_first(query_t), heads_first(all_keys), heads_first(all_values))
    )
    context_b_t = ctx_heads.reshape(width, -1).astype(bf16)
    z_one = x.astype(single_float) + contract_dims(context_b_t, wo_full, 0, 0) + bo
    n_one, rstd_one = normalize(z_one)
    x_one = n_one * g1 + c1
    x_one_b = x_one.astype(bf16)
    upper = jnp.dot(x_one_b, wu_full, preferred_element_type=single_float) + bu
    hidden_f, gelu_back = jax.vjp(gelu_exact, upper)
    hidden = hidden_f.astype(bf16)
    z_two = x_one + jnp.dot(hidden, wd_full, preferred_element_type=single_float) + bd
    n_two, rstd_two = normalize(z_two)
    out = (n_two * g2 + c2).astype(bf16)
    wq_back, wo_back, wu_back, wd_back = (wq_full, wo_full, wu_full, wd_full)
    keys_b, values_b = (all_keys, all_values)
    grad = cotangent[0].astype(single_float)
    dg_two = jnp.sum(grad * n_two, axis=0)
    db_two = jnp.sum(grad, axis=0)
    dz_two = norm_back(grad * g2, n_two, rstd_two)
    dz_two_b = dz_two.astype(bf16)
    dw_down = contract_dims(hidden, dz_two_b, 0, 0)
    db_down = jnp.sum(dz_two, axis=0)
    dhid = contract_dims(dz_two_b, wd_back, 1, 1)
    dupper = gelu_back(dhid)[0]
    dupper_b = dupper.astype(bf16)
    dw_up = contract_dims(x_one_b, dupper_b, 0, 0)
    db_up = jnp.sum(dupper, axis=0)
    dx_one = dz_two + contract_dims(dupper_b, wu_back, 1, 1)
    dg_one = jnp.sum(dx_one * n_one, axis=0)
    db_one = jnp.sum(dx_one, axis=0)
    dz_one = norm_back(dx_one * g1, n_one, rstd_one)
    dz_one_b = dz_one.astype(bf16)
    dw_out = contract_dims(context_b_t, dz_one_b, 1, 0)
    db_out = jnp.sum(dz_one, axis=0)
    dctx_t = contract_dims(wo_back, dz_one_b, 1, 1)
    dctx_b_t = dctx_t.astype(bf16)
    delta = jnp.sum(heads_first(dctx_t) * ctx_heads, axis=1)
    qh = heads_first(query_t)

    def head_bwd(operations):
        query_index, key_index, value_index, lse_index, context_grad_index, delta_index = operations
        scores = contract_dims(query_index, key_index, 0, 0) * scale
        scores = jnp.where(valid[None, :], scores, -1e30)
        prob = jnp.exp(scores - lse_index[:, None])
        block_probs = prob.astype(bf16)
        value_gradient = contract_dims(context_grad_index, block_probs, 1, 0)
        prob_gradient = contract_dims(context_grad_index, value_index, 0, 0)
        dscore = (prob * (prob_gradient - delta_index[:, None])).astype(bf16)
        query_gradient = contract_dims(key_index, dscore, 1, 1) * scale
        key_gradient = contract_dims(query_index, dscore, 1, 0) * scale
        return (query_gradient, key_gradient, value_gradient)

    dqh, dkh, dvh = lax.map(
        head_bwd,
        (qh, heads_first(keys_b), heads_first(values_b), lse_all, heads_first(dctx_b_t), delta),
    )
    key_grad_t, value_grad_t = (
        lax.psum_scatter(
            dkh.reshape(width, -1).astype(jnp.bfloat16), "ctx", scatter_dimension=1, tiled=True
        ).astype(jnp.float32),
        lax.psum_scatter(
            dvh.reshape(width, -1).astype(jnp.bfloat16), "ctx", scatter_dimension=1, tiled=True
        ).astype(jnp.float32),
    )
    query_grad_t = dqh.reshape(width, -1)
    dqkv_b_t = jnp.concatenate([query_grad_t, key_grad_t, value_grad_t], axis=0).astype(bf16)
    dw_qkv = contract_dims(x, dqkv_b_t, 0, 1)
    dx = dz_one + contract_dims(dqkv_b_t, wq_back, 0, 1)
    grads = (
        dw_qkv,
        jnp.sum(query_grad_t, axis=1),
        jnp.sum(value_grad_t, axis=1),
        dw_out,
        db_out,
        dg_one,
        db_one,
        dw_up,
        db_up,
        dw_down,
        db_down,
        dg_two,
        db_two,
    )
    pieces = (
        lax.psum_scatter(
            grads[0].astype(jnp.bfloat16), "shard", scatter_dimension=0, tiled=True
        ).astype(jnp.float32),
        lax.psum_scatter(
            grads[1].astype(jnp.bfloat16), "shard", scatter_dimension=0, tiled=True
        ).astype(jnp.float32),
        lax.psum_scatter(
            grads[2].astype(jnp.bfloat16), "shard", scatter_dimension=0, tiled=True
        ).astype(jnp.float32),
        lax.psum_scatter(
            grads[3].astype(jnp.bfloat16), "shard", scatter_dimension=0, tiled=True
        ).astype(jnp.float32),
        lax.psum_scatter(
            grads[4].astype(jnp.bfloat16), "shard", scatter_dimension=0, tiled=True
        ).astype(jnp.float32),
        lax.psum_scatter(
            grads[5].astype(jnp.bfloat16), "shard", scatter_dimension=0, tiled=True
        ).astype(jnp.float32),
        lax.psum_scatter(
            grads[6].astype(jnp.bfloat16), "shard", scatter_dimension=0, tiled=True
        ).astype(jnp.float32),
        lax.psum_scatter(
            grads[7].astype(jnp.bfloat16), "shard", scatter_dimension=0, tiled=True
        ).astype(jnp.float32),
        lax.psum_scatter(
            grads[8].astype(jnp.bfloat16), "shard", scatter_dimension=0, tiled=True
        ).astype(jnp.float32),
        lax.psum_scatter(
            grads[9].astype(jnp.bfloat16), "shard", scatter_dimension=0, tiled=True
        ).astype(jnp.float32),
        lax.psum_scatter(
            grads[10].astype(jnp.bfloat16), "shard", scatter_dimension=0, tiled=True
        ).astype(jnp.float32),
        lax.psum_scatter(
            grads[11].astype(jnp.bfloat16), "shard", scatter_dimension=0, tiled=True
        ).astype(jnp.float32),
        lax.psum_scatter(
            grads[12].astype(jnp.bfloat16), "shard", scatter_dimension=0, tiled=True
        ).astype(jnp.float32),
    )
    summed = (
        lax.psum(pieces[0].astype(jnp.bfloat16), "ctx").astype(jnp.float32),
        lax.psum(pieces[1].astype(jnp.bfloat16), "ctx").astype(jnp.float32),
        lax.psum(pieces[2].astype(jnp.bfloat16), "ctx").astype(jnp.float32),
        lax.psum(pieces[3].astype(jnp.bfloat16), "ctx").astype(jnp.float32),
        lax.psum(pieces[4].astype(jnp.bfloat16), "ctx").astype(jnp.float32),
        lax.psum(pieces[5].astype(jnp.bfloat16), "ctx").astype(jnp.float32),
        lax.psum(pieces[6].astype(jnp.bfloat16), "ctx").astype(jnp.float32),
        lax.psum(pieces[7].astype(jnp.bfloat16), "ctx").astype(jnp.float32),
        lax.psum(pieces[8].astype(jnp.bfloat16), "ctx").astype(jnp.float32),
        lax.psum(pieces[9].astype(jnp.bfloat16), "ctx").astype(jnp.float32),
        lax.psum(pieces[10].astype(jnp.bfloat16), "ctx").astype(jnp.float32),
        lax.psum(pieces[11].astype(jnp.bfloat16), "ctx").astype(jnp.float32),
        lax.psum(pieces[12].astype(jnp.bfloat16), "ctx").astype(jnp.float32),
    )
    return (
        out[None],
        dx[None],
        summed[0],
        summed[1],
        summed[2],
        summed[3],
        summed[4],
        summed[5],
        summed[6],
        summed[7],
        summed[8],
        summed[9],
        summed[10],
        summed[11],
        summed[12],
    )


def solution(mesh):
    in_specs = (
        P("shard", "ctx", None),
        P("shard"),
        P("shard", "ctx", None),
        P("shard", None),
        P("shard"),
        P("shard"),
        P("shard", None),
        P("shard"),
        P("shard"),
        P("shard"),
        P("shard", None),
        P("shard"),
        P("shard", None),
        P("shard"),
        P("shard"),
        P("shard"),
    )
    out_specs = (
        P("shard", "ctx", None),
        P("shard", "ctx", None),
        P("shard", None),
        P("shard"),
        P("shard"),
        P("shard", None),
        P("shard"),
        P("shard"),
        P("shard"),
        P("shard", None),
        P("shard"),
        P("shard", None),
        P("shard"),
        P("shard"),
        P("shard"),
    )
    return jax.shard_map(local, mesh=mesh, in_specs=in_specs, out_specs=out_specs, check_vma=False)
```

profile of v0, /device:TPU:0, one launch (start us, length us, event | category | flops | bytes accessed | tf_op | source)
XLA Modules:
  0.0 760.2 jit_solution(821553112586905481)
XLA Ops:
  15.8 18.3 %all-reduce.20 = (bf16[768]{0:T(1024)(128)(2,1)S(1)}, bf16[768]{0:T(1024)(128)(2,1)S(1)}, bf16[768]{0:T(1024)(128)(2,1)S(1)}, bf16[768]{0:T(1024)(128)(2,1)S(1)}...) all-reduce(bf16[768]{0:T(1024)(128)(2,1)S(1)} %dynamic-update-slice, ...), channel_id=1, replica_groups=mesh['shard'=4,'ctx'=8] {'shard'}, use_global_device_ids=true, to_apply=%add.1 | all-reduce | flops 5376 | bytes 21504
  34.1 25.7 %all-gather.8.cloned.1.call-done = bf16[768,2304]{1,0:T(8,128)(2,1)} async-done(((bf16[192,2304]{1,0:T(8,128)(2,1)}), bf16[768,2304]{1,0:T(8,128)(2,1)}) %all-gather.8.cloned.1.call-update) | async-done | bytes 3538960 | tf_op jit(solution)/shard_map/all_gather | solution.py:60
  59.8 3.1 fusion.71
  66.6 8.3 %all-gather = bf16[4,1,768]{2,1,0:T(2,128)(2,1)S(1)} all-gather(bf16[1,1,768]{2,1,0:T(2,128)(2,1)S(1)} %reshape.174), channel_id=1, replica_groups=mesh['shard'=4,'ctx'=8] {'shard'}, dimensions={0}, use_global_device_ids=true | all-gather | bytes 7680 | tf_op jit(solution)/shard_map/all_gather | solution.py:68
  74.9 16.2 %all-gather.10.cloned.1.call-done = bf16[768,1024]{1,0:T(8,128)(2,1)} async-done(((bf16[768,128]{1,0:T(8,128)(2,1)}), bf16[768,1024]{1,0:T(8,128)(2,1)}) %all-gather.10.cloned.1.call-update) | async-done | bytes 1572880 | tf_op jit(solution)/shard_map/all_gather | solution.py:101
  91.2 28.1 %all-gather.12.cloned.1.call-done = bf16[768,1024]{1,0:T(8,128)(2,1)} async-done(((bf16[768,128]{1,0:T(8,128)(2,1)}), bf16[768,1024]{1,0:T(8,128)(2,1)}) %all-gather.12.cloned.1.call-update) | async-done | bytes 1572880 | tf_op jit(solution)/shard_map/all_gather | solution.py:100
  119.3 55.8 %while.28 = (s32[]{:T(128)}, f32[12,64,128]{2,1,0:T(8,128)S(1)}, f32[12,128]{1,0:T(8,128)}, bf16[12,64,1024]{2,1,0:T(8,128)(2,1)}, bf16[12,64,128]{2,1,0:T(8,128...) while((s32[]{:T(128)}, f32[12,64,128]{2,1,0:T(8,128)S(1)}, ...), condition=%wide.region_3.4_spmd.clone, body=%wide.region_0.3_spmd.clone.sunk | while | flops 34472832 | bytes 1892965 | solution.py:115
  177.2 28.8 %all-gather.16.cloned.1.call-done = bf16[768,3072]{1,0:T(8,128)(2,1)} async-done(((bf16[192,3072]{1,0:T(8,128)(2,1)}), bf16[768,3072]{1,0:T(8,128)(2,1)}) %all-gather.16.cloned.1.call-update) | async-done | bytes 4718608 | tf_op jit(solution)/shard_map/all_gather | solution.py:67
  206.0 7.6 %multiply_convert_fusion = (bf16[128,3072]{1,0:T(8,128)(2,1)S(1)}, f32[128,3072]{1,0:T(8,128)}) fusion(f32[3072]{0:T(1024)S(1)} %bitcast.162, bf16[768,3072]{1,0:T(8,128)(2,1)} %all-gather.16.cloned.1.call-done, f32[128,768]{1,0:T(8,128)S(1)} %get-tuple-element.303, f32[768]{0:T(1024)S(1)} %convert_element_type.209, f32[768]{0:T(1024)S(1)} %convert_element_type.208, ...), kind=kOutput, calls=%fused_computation.67 | convolution fusion | flops 630423552 | bytes 7490560 | tf_op jit(solution)/shard_map/dot_general | solution.py:123
  213.7 51.0 %all-gather.18.cloned.1.call-done = bf16[3072,768]{1,0:T(8,128)(2,1)} async-done(((bf16[768,768]{1,0:T(8,128)(2,1)}), bf16[3072,768]{1,0:T(8,128)(2,1)}) %all-gather.18.cloned.1.call-update) | async-done | bytes 4718608 | tf_op jit(solution)/shard_map/all_gather | solution.py:69
  264.7 3.4 fusion.91
  269.9 5.5 fusion.93
  275.4 2.4 multiply_reduce_fusion
  286.0 87.0 %while.29 = (s32[]{:T(128)}, f32[12,64,128]{2,1,0:T(8,128)S(1)}, bf16[12,64,1024]{2,1,0:T(8,128)(2,1)}, bf16[12,64,1024]{2,1,0:T(8,128)(2,1)}, bf16[12,64,1024]{...) while((s32[]{:T(128)}, f32[12,64,128]{2,1,0:T(8,128)S(1)}, ...), condition=%wide.region_14.15_spmd.clone, body=%wide.region_13.14_spmd.clone.sunk | while | flops 84878336 | bytes 3385469 | solution.py:168
  373.0 2.6 copy.40
  375.7 2.6 copy.42
  379.3 30.6 %reduce-scatter.19.cloned.1.call-done = bf16[128,768]{1,0:T(8,128)(2,1)} async-done(((bf16[1024,768]{1,0:T(8,128)(2,1)}), bf16[128,768]{1,0:T(8,128)(2,1)}) %reduce-scatter.19.cloned.1.call-update) | async-done | bytes 196624
  411.0 34.3 %reduce-scatter.21.cloned.1.call-done = bf16[128,768]{1,0:T(8,128)(2,1)} async-done(((bf16[1024,768]{1,0:T(8,128)(2,1)}), bf16[128,768]{1,0:T(8,128)(2,1)}) %reduce-scatter.21.cloned.1.call-update) | async-done | bytes 196624
  446.5 2.8 fusion.47
  449.3 5.8 copy.44
  457.6 3.7 convolution_convert_fusion.1
  461.3 3.6 convolution_convert_fusion
  465.0 35.7 %reduce-scatter.23.cloned.1.call-done = bf16[192,2304]{1,0:T(8,128)(2,1)} async-done(((bf16[768,2304]{1,0:T(8,128)(2,1)}), bf16[192,2304]{1,0:T(8,128)(2,1)}) %reduce-scatter.23.cloned.1.call-update) | async-done | bytes 884752
  500.7 2.3 copy.45
  503.0 29.7 %reduce-scatter.13.cloned.1.call-done = bf16[192,768]{1,0:T(8,128)(2,1)} async-done(((bf16[768,768]{1,0:T(8,128)(2,1)}), bf16[192,768]{1,0:T(8,128)(2,1)}) %reduce-scatter.13.cloned.1.call-update) | async-done | bytes 294928 | tf_op jit(solution)/shard_map/reduce_scatter | solution.py:209
  532.8 60.0 %reduce-scatter.15.cloned.1.call-done = bf16[192,3072]{1,0:T(8,128)(2,1)} async-done(((bf16[768,3072]{1,0:T(8,128)(2,1)}), bf16[192,3072]{1,0:T(8,128)(2,1)}) %reduce-scatter.15.cloned.1.call-update) | async-done | bytes 1179664 | tf_op jit(solution)/shard_map/reduce_scatter | solution.py:221
  592.8 59.8 %reduce-scatter.17.cloned.1.call-done = bf16[768,768]{1,0:T(8,128)(2,1)} async-done(((bf16[3072,768]{1,0:T(8,128)(2,1)}), bf16[768,768]{1,0:T(8,128)(2,1)}) %reduce-scatter.17.cloned.1.call-update) | async-done | bytes 1179664 | tf_op jit(solution)/shard_map/reduce_scatter | solution.py:227
  659.2 16.7 %all-reduce.19 = (bf16[768]{0:T(1024)(128)(2,1)}, bf16[768]{0:T(1024)(128)(2,1)}, bf16[768]{0:T(1024)(128)(2,1)}, bf16[768]{0:T(1024)(128)(2,1)}, bf16[768]{0:T(...) all-reduce(bf16[768]{0:T(1024)(128)(2,1)} %dynamic-update-slice.7, ...), channel_id=1, replica_groups=mesh['shard'=4,'ctx'=8] {'shard'}, use_global_device_ids=true, to_apply=%add.7 | all-reduce | flops 9984 | bytes 39936
  686.7 15.6 %all-reduce.17 = (bf16[192]{0:T(256)(128)(2,1)}, bf16[192]{0:T(256)(128)(2,1)}, bf16[192]{0:T(256)(128)(2,1)}, bf16[192]{0:T(256)(128)(2,1)}, bf16[192]{0:T(256)...) all-reduce(bf16[192]{0:T(256)(128)(2,1)} %dynamic-slice.9, ...), channel_id=1, replica_groups=mesh['shard'=4,'ctx'=8] {'ctx'}, use_global_device_ids=true, to_apply=%region_21.22 | all-reduce | flops 2304 | bytes 9216 | tf_op jit(solution)/shard_map/psum | solution.py:242
  715.0 3.3 fusion.55
  718.3 28.3 %all-reduce.23.cloned.1.call-done = (bf16[192,2304]{0,1:T(8,128)(2,1)}, bf16[192,768]{1,0:T(8,128)(2,1)}, bf16[192,3072]{1,0:T(8,128)(2,1)}, bf16[768,768]{1,0:T(8,128)(2,1)}) async-done(((bf16[192,2304]{0,1:T(8,128)(2,1)}, bf16[192,768]{1,0:T(8,128)(2,1)}, bf16[192,3072]{1,0:T(8,128)(2,1)}, bf16[768,768]{1,0:T(8,128)(2,1)}), (bf16[192,2304]{0,1:T(8,128)(2,1)}, bf16[192,768]{1,0:T(8,128)(2,1)}, ...) | async-done | bytes 3538960 | tf_op jit(solution)/shard_map/psum | solution.py:241
  746.6 3.0 convert_element_type.243
  (317 shorter events, 204.1 us)
Async XLA Ops:
  7.2 52.7 %all-gather.8.cloned.1.call-start = ((), (), s32[]{:S(2)}) async-start(), calls=%async_computation.6 | async-start | bytes 4423680 | tf_op jit(solution)/shard_map/all_gather | solution.py:60
  7.9 83.3 %all-gather.10.cloned.1.call-start = ((), (), s32[]{:S(2)}) async-start(), calls=%async_computation.7 | async-start | bytes 1769472 | tf_op jit(solution)/shard_map/all_gather | solution.py:101
  63.9 2.6 copy-start.22
  63.9 55.3 %all-gather.12.cloned.1.call-start = ((), (), s32[]{:S(2)}) async-start(), calls=%async_computation.8 | async-start | bytes 1769472 | tf_op jit(solution)/shard_map/all_gather | solution.py:100
  64.7 110.5 %all-gather.14.cloned.1.call-start = ((), (), s32[]{:S(2)}) async-start(), calls=%async_computation.9 | async-start | bytes 1474560 | tf_op jit(solution)/shard_map/all_gather | solution.py:63
  65.3 140.8 %all-gather.16.cloned.1.call-start = ((), (), s32[]{:S(2)}) async-start(), calls=%async_computation.10 | async-start | bytes 5898240 | tf_op jit(solution)/shard_map/all_gather | solution.py:67
  65.9 198.8 %all-gather.18.cloned.1.call-start = ((), (), s32[]{:S(2)}) async-start(), calls=%async_computation.11 | async-start | bytes 5898240 | tf_op jit(solution)/shard_map/all_gather | solution.py:69
  66.5 343.5 %reduce-scatter.19.cloned.1.call-start = ((), (), s32[]{:S(2)}) async-start(), calls=%async_computation.15 | async-start | bytes 1769472
  119.3 55.9 %copy-start.5 = (bf16[1,128,768]{2,1,0:T(8,128)(2,1)S(1)}, bf16[1,128,768]{2,1,0:T(8,128)(2,1)}, u32[]{:S(2)}) copy-start(bf16[1,128,768]{2,1,0:T(8,128)(2,1)} %param.20) | copy-start | bytes 589828
  175.2 38.5 %copy-start.9 = (bf16[12,64,128]{2,1,0:T(8,128)(2,1)}, bf16[12,64,128]{2,1,0:T(8,128)(2,1)S(1)}, u32[]{:S(2)}) copy-start(bf16[12,64,128]{2,1,0:T(8,128)(2,1)S(1)} %convert_element_type.205) | copy-start | bytes 589828
  177.2 98.2 %copy-start.16 = (f32[128]{0:T(128)}, f32[128]{0:T(128)S(1)}, u32[]{:S(2)}) copy-start(f32[128]{0:T(128)S(1)} %add_rsqrt_fusion.1) | copy-start | bytes 1540
  264.7 3.6 copy-start.11
  264.7 5.2 copy-start.3
  268.1 7.3 copy-start.18
  268.3 7.1 copy-start.21
  269.1 6.3 slice-start
  269.9 5.5 slice-start.1
  279.3 175.9 %copy-start.2 = (f32[128,768]{1,0:T(8,128)}, f32[128,768]{1,0:T(8,128)S(1)}, u32[]{:S(2)}) copy-start(f32[128,768]{1,0:T(8,128)S(1)} %get-tuple-element.291) | copy-start | bytes 1179652
  375.6 69.7 %reduce-scatter.21.cloned.1.call-start = ((), (), s32[]{:S(2)}) async-start(), calls=%async_computation.16 | async-start | bytes 1769472
  378.3 122.4 %reduce-scatter.23.cloned.1.call-start = ((), (), s32[]{:S(2)}) async-start(), calls=%async_computation.17 | async-start | bytes 4423680
  379.3 70.0 %copy-start.8 = (bf16[12,64,128]{2,1,0:T(8,128)(2,1)}, bf16[12,64,128]{2,1,0:T(8,128)(2,1)S(1)}, u32[]{:S(2)}) copy-start(bf16[12,64,128]{2,1,0:T(8,128)(2,1)S(1)} %get-tuple-element.298) | copy-start | bytes 589828
  411.0 38.3 %copy-start.6 = (bf16[768,128]{1,0:T(8,128)(2,1)}, bf16[768,128]{1,0:T(8,128)(2,1)S(1)}, u32[]{:S(2)}) copy-start(bf16[768,128]{1,0:T(8,128)(2,1)S(1)} %copy.41) | copy-start | bytes 589828
  446.4 2.9 copy-start.7
  455.1 77.6 %reduce-scatter.13.cloned.1.call-start = ((), (), s32[]{:S(2)}) async-start(), calls=%async_computation.12 | async-start | bytes 1474560 | tf_op jit(solution)/shard_map/reduce_scatter | solution.py:209
  457.5 135.3 %reduce-scatter.15.cloned.1.call-start = ((), (), s32[]{:S(2)}) async-start(), calls=%async_computation.13 | async-start | bytes 5898240 | tf_op jit(solution)/shard_map/reduce_scatter | solution.py:221
  461.3 191.4 %reduce-scatter.17.cloned.1.call-start = ((), (), s32[]{:S(2)}) async-start(), calls=%async_computation.14 | async-start | bytes 5898240 | tf_op jit(solution)/shard_map/reduce_scatter | solution.py:227
  464.9 281.7 %all-reduce.23.cloned.1.call-start = ((), (), s32[]{:S(2)}) async-start(), calls=%async_computation.18 | async-start | bytes 7667712 | tf_op jit(solution)/shard_map/psum | solution.py:241
  652.6 5.0 copy-start.15
  652.6 6.6 copy-start.20
  652.6 60.5 %copy-start.19 = (f32[128]{0:T(128)S(1)}, f32[128]{0:T(128)}, u32[]{:S(2)}) copy-start(f32[128]{0:T(128)} %copy-done.18) | copy-start | bytes 1540
  652.6 62.3 %copy-start = (bf16[768,2304]{1,0:T(8,128)(2,1)S(1)}, bf16[768,2304]{1,0:T(8,128)(2,1)}, u32[]{:S(2)}) copy-start(bf16[768,2304]{1,0:T(8,128)(2,1)} %all-gather.8.cloned.1.call-done) | copy-start | bytes 10616836
  746.6 3.0 copy-start.12
  (7 other events, 11.1 us)
Sparse Core Ops, SparseCore 0:
  9.8 49.9 all-gather.7
  64.0 27.0 all-gather.9
  93.3 25.8 all-gather.11
  121.0 26.3 all-gather.13
  149.1 56.9 all-gather.15
  207.7 56.9 all-gather.17
  375.7 34.1 reduce-scatter.18
  412.8 32.5 reduce-scatter.20
  455.2 45.4 reduce-scatter.22
  504.1 28.6 reduce-scatter.12
  535.8 56.9 reduce-scatter.14
  595.6 56.9 reduce-scatter.16
  655.8 90.7 all-reduce.22
where the time goes:
time: 764 us; the launch traced here: 760 us
  waiting for transfers between devices  431 us (56%)
  matrix products  140 us (18%)
  local copies, waits for them, and re-layouts  66.7 us (9%)
  blocking collectives  58.9 us (8%)
  other arithmetic  46.2 us (6%)
  between operations  16.2 us (2%)
    dot_general x94, matrix products, contract_dims(): lax.dot_general(left, right, (((left_dim,), (right_dim,)), ((), ())), pre...  129 us
    unnamed x16, waiting for transfers between devices  103 us
    reduce_scatter x1, waiting for transfers between devices, local(): lax.psum_scatter(grads[7].astype(jnp.bfloat16), 'shard', scatter_dimensio...  60 us
    reduce_scatter x1, waiting for transfers between devices, local(): lax.psum_scatter(grads[9].astype(jnp.bfloat16), 'shard', scatter_dimensio...  59.8 us
    all_gather x1, waiting for transfers between devices, local(): lax.all_gather(w_down, 'shard', axis=0, tiled=True)  51 us
    unnamed x86, local copies, waits for them, and re-layouts  37.9 us
    unnamed x2, blocking collectives  35 us
    reduce_scatter x1, waiting for transfers between devices, local(): lax.psum_scatter(grads[3].astype(jnp.bfloat16), 'shard', scatter_dimensio...  29.7 us
  transfers between devices with their start and end apart: 13, of which 12 were waited for; matrix products, arithmetic and copies ran while one was open for 16% of the time, Pallas kernels for 0%

commit v1 on v0

--- a/solution.py
+++ b/solution.py
@@ -6,6 +6,26 @@
 
 HEADS = 12
 EPS = 1e-06
+
+
+def _supply_all_views(sample, dim_i):
+    heard = list(sample.shape[1:])
+    heard[dim_i] *= sample.shape[0]
+    block_next = jnp.moveaxis(sample, 0, dim_i).reshape(heard)
+    return block_next
+
+
+def refer_sectors_here(block_here, chip_axis):
+    axis_total = lax.axis_size(chip_axis)
+    f_now = block_here[None]
+    for tick in range(axis_total.bit_length() - 1):
+        x_next = 1 << tick
+        v_next = tuple(((q, q ^ x_next) for q in range(axis_total)))
+        tile_out = lax.ppermute(f_now, chip_axis, perm=v_next)
+        h_now = jnp.stack([f_now, tile_out], 0)
+        raw_out = lax.axis_index(chip_axis) >> tick & 1
+        f_now = jnp.where(raw_out == 0, h_now, h_now[::-1]).reshape(-1, *block_here.shape)
+    return f_now
 
 
 def normalize(z):
@@ -56,6 +76,12 @@
 ):
     single_float = jnp.float32
     bf16 = jnp.bfloat16
+
+    def move_the_plate(x_local, frame, array_axis):
+        newest = refer_sectors_here(x_local, frame)
+        left_arr = _supply_all_views(newest, array_axis)
+        return left_arr
+
     full = (
         lax.all_gather(w_qkv, "shard", axis=0, tiled=True),
         lax.all_gather(b_query, "shard", axis=0, tiled=True),
@@ -66,7 +92,7 @@
         lax.all_gather(ln1_bias, "shard", axis=0, tiled=True),
         lax.all_gather(w_up, "shard", axis=0, tiled=True),
         lax.all_gather(b_up, "shard", axis=0, tiled=True),
-        lax.all_gather(w_down, "shard", axis=0, tiled=True),
+        move_the_plate(w_down, "shard", 0),
         lax.all_gather(b_down, "shard", axis=0, tiled=True),
         lax.all_gather(ln2_gain, "shard", axis=0, tiled=True),
         lax.all_gather(ln2_bias, "shard", axis=0, tiled=True),

time: 764 us -> 703 us (0.920)
  waiting for transfers between devices: 431 us -> 360 us
  blocking collectives: 58.9 us -> 111 us
  local copies, waits for them, and re-layouts: 66.7 us -> 31.4 us
    all_gather x1, blocking collectives: 8.3 us -> 62.7 us  [local(): lax.all_gather(b_up, 'shard', axis=0, tiled=True)]
    all_gather x1 -> x0, waiting for transfers between devices: 51 us -> none  [local(): lax.all_gather(w_down, 'shard', axis=0, tiled=True)]
    all_gather x1, waiting for transfers between devices: 28.1 us -> 0.01 us  [local(): lax.all_gather(keys_t, 'ctx', axis=1, tiled=True)]
    ppermute x0 -> x2, waiting for transfers between devices: none -> 26.1 us  [refer_sectors_here(): tile_out = lax.ppermute(f_now, chip_axis, perm=v_next)]
    all_gather x1, waiting for transfers between devices: 28.8 us -> 5.74 us  [local(): lax.all_gather(w_up, 'shard', axis=0, tiled=True)]
    psum x1, waiting for transfers between devices: 28.3 us -> 50.1 us  [local(): lax.psum(pieces[0].astype(jnp.bfloat16), 'ctx').astype(jnp.float32)]
    all_gather x1, waiting for transfers between devices: 16.2 us -> 0.01 us  [local(): lax.all_gather(values_t, 'ctx', axis=1, tiled=True)]
    dynamic_update_slice x12, local copies, waits for them, and re-layouts: 15.4 us -> 0.45 us  [local(): lax.map(head_fwd, (heads_first(query_t), heads_first(all_keys), heads_fir...]
  transfers between devices with their start and end apart: 13 -> 14, of which waited for: 12 -> 10; matrix products, arithmetic and copies ran while one was open for 16% -> 12% of each run, Pallas kernels for 0% -> 0%
where the time goes in v1:
time: 703 us; the launch traced here: 700 us
  waiting for transfers between devices  360 us (51%)
  matrix products  136 us (19%)
  blocking collectives  111 us (16%)
  other arithmetic  39.7 us (6%)
  local copies, waits for them, and re-layouts  31.4 us (4%)
  between operations  16.7 us (2%)
    dot_general x94, matrix products, contract_dims(): lax.dot_general(left, right, (((left_dim,), (right_dim,)), ((), ())), pre...  129 us
    unnamed x15, waiting for transfers between devices  103 us
    all_gather x1, blocking collectives, local(): lax.all_gather(b_up, 'shard', axis=0, tiled=True)  62.7 us
    reduce_scatter x1, waiting for transfers between devices, local(): lax.psum_scatter(grads[9].astype(jnp.bfloat16), 'shard', scatter_dimensio...  60 us
    reduce_scatter x1, waiting for transfers between devices, local(): lax.psum_scatter(grads[7].astype(jnp.bfloat16), 'shard', scatter_dimensio...  59.9 us
    psum x1, waiting for transfers between devices, local(): lax.psum(pieces[0].astype(jnp.bfloat16), 'ctx').astype(jnp.float32)  50.1 us
    unnamed x2, blocking collectives  33.7 us
    reduce_scatter x1, waiting for transfers between devices, local(): lax.psum_scatter(grads[3].astype(jnp.bfloat16), 'shard', scatter_dimensio...  29.9 us
  transfers between devices with their start and end apart: 14, of which 10 were waited for; matrix products, arithmetic and copies ran while one was open for 12% of the time, Pallas kernels for 0%

profile of v1, /device:TPU:0, one launch (start us, length us, event | category | flops | bytes accessed | tf_op | source)
XLA Modules:
  0.0 700.4 jit_solution(10304759340301452412)
XLA Ops:
  15.8 18.3 %all-reduce.20 = (bf16[768]{0:T(1024)(128)(2,1)S(1)}, bf16[768]{0:T(1024)(128)(2,1)S(1)}, bf16[768]{0:T(1024)(128)(2,1)S(1)}, bf16[768]{0:T(1024)(128)(2,1)S(1)}...) all-reduce(bf16[768]{0:T(1024)(128)(2,1)S(1)} %dynamic-update-slice, ...), channel_id=1, replica_groups=mesh['shard'=4,'ctx'=8] {'shard'}, use_global_device_ids=true, to_apply=%add.1 | all-reduce | flops 5376 | bytes 21504
  34.1 25.7 %all-gather.7.cloned.1.call-done = bf16[768,2304]{1,0:T(8,128)(2,1)} async-done(((bf16[192,2304]{1,0:T(8,128)(2,1)}), bf16[768,2304]{1,0:T(8,128)(2,1)}) %all-gather.7.cloned.1.call-update) | async-done | bytes 3538960 | tf_op jit(solution)/shard_map/all_gather | solution.py:86
  59.8 3.1 fusion.73
  66.3 26.1 %collective-permute-done = bf16[1,768,768]{2,1,0:T(8,128)(2,1)S(1)} collective-permute-done((bf16[1,768,768]{2,1,0:T(8,128)(2,1)S(1)}, bf16[1,768,768]{2,1,0:T(8,128)(2,1)S(1)}, u32[]{:S(2)}, u32[]{:S(2)}) %collective-permute-start) | collective-permute-done | bytes 1179680 | tf_op jit(solution)/shard_map/ppermute | solution.py:24
  92.6 1.9 fusion.49
  96.7 62.7 %all-gather = bf16[4,1,768]{2,1,0:T(2,128)(2,1)S(1)} all-gather(bf16[1,1,768]{2,1,0:T(2,128)(2,1)S(1)} %reshape.178), channel_id=1, replica_groups=mesh['shard'=4,'ctx'=8] {'shard'}, dimensions={0}, use_global_device_ids=true | all-gather | bytes 7680 | tf_op jit(solution)/shard_map/all_gather | solution.py:94
  159.5 2.1 pad_maximum_fusion
  161.6 3.1 reverse_select_fusion
  164.8 41.1 %while.28 = (s32[]{:T(128)}, f32[12,64,128]{2,1,0:T(8,128)S(1)}, f32[12,128]{1,0:T(8,128)S(1)}, bf16[12,64,1024]{2,1,0:T(8,128)(2,1)}, bf16[12,64,128]{2,1,0:T(8...) while((s32[]{:T(128)}, f32[12,64,128]{2,1,0:T(8,128)S(1)}, ...), condition=%wide.region_3.4_spmd.clone, body=%wide.region_0.3_spmd.clone.sunk | while | flops 34472832 | bytes 1892965 | solution.py:141
  208.5 5.7 all-gather.15.cloned.1.call-done
  214.3 6.0 multiply_convert_fusion
  221.9 4.9 fusion.95
  233.6 78.9 %while.29 = (s32[]{:T(128)}, f32[12,64,128]{2,1,0:T(8,128)S(1)}, bf16[12,64,1024]{2,1,0:T(8,128)(2,1)}, bf16[12,64,1024]{2,1,0:T(8,128)(2,1)}, bf16[12,64,1024]{...) while((s32[]{:T(128)}, f32[12,64,128]{2,1,0:T(8,128)S(1)}, ...), condition=%wide.region_14.15_spmd.clone, body=%wide.region_13.14_spmd.clone.sunk | while | flops 84878336 | bytes 3385469 | solution.py:194
  312.6 2.6 copy.40
  315.2 2.6 copy.42
  318.3 31.3 %reduce-scatter.19.cloned.1.call-done = bf16[128,768]{1,0:T(8,128)(2,1)} async-done(((bf16[1024,768]{1,0:T(8,128)(2,1)}), bf16[128,768]{1,0:T(8,128)(2,1)}) %reduce-scatter.19.cloned.1.call-update) | async-done | bytes 196624
  350.7 34.4 %reduce-scatter.21.cloned.1.call-done = bf16[128,768]{1,0:T(8,128)(2,1)} async-done(((bf16[1024,768]{1,0:T(8,128)(2,1)}), bf16[128,768]{1,0:T(8,128)(2,1)}) %reduce-scatter.21.cloned.1.call-update) | async-done | bytes 196624
  386.2 2.8 fusion.47
  389.0 5.8 copy.44
  394.9 2.5 convolution_convert_fusion.3
  397.4 3.6 convolution_convert_fusion.1
  401.1 3.6 convolution_convert_fusion
  404.8 35.7 %reduce-scatter.23.cloned.1.call-done = bf16[192,2304]{1,0:T(8,128)(2,1)} async-done(((bf16[768,2304]{1,0:T(8,128)(2,1)}), bf16[192,2304]{1,0:T(8,128)(2,1)}) %reduce-scatter.23.cloned.1.call-update) | async-done | bytes 884752
  440.5 2.3 copy.45
  442.8 29.9 %reduce-scatter.13.cloned.1.call-done = bf16[192,768]{1,0:T(8,128)(2,1)} async-done(((bf16[768,768]{1,0:T(8,128)(2,1)}), bf16[192,768]{1,0:T(8,128)(2,1)}) %reduce-scatter.13.cloned.1.call-update) | async-done | bytes 294928 | tf_op jit(solution)/shard_map/reduce_scatter | solution.py:235
  472.7 59.9 %reduce-scatter.15.cloned.1.call-done = bf16[192,3072]{1,0:T(8,128)(2,1)} async-done(((bf16[768,3072]{1,0:T(8,128)(2,1)}), bf16[192,3072]{1,0:T(8,128)(2,1)}) %reduce-scatter.15.cloned.1.call-update) | async-done | bytes 1179664 | tf_op jit(solution)/shard_map/reduce_scatter | solution.py:247
  532.6 60.0 %reduce-scatter.17.cloned.1.call-done = bf16[768,768]{1,0:T(8,128)(2,1)} async-done(((bf16[3072,768]{1,0:T(8,128)(2,1)}), bf16[768,768]{1,0:T(8,128)(2,1)}) %reduce-scatter.17.cloned.1.call-update) | async-done | bytes 1179664 | tf_op jit(solution)/shard_map/reduce_scatter | solution.py:253
  595.2 15.4 %all-reduce.19 = (bf16[768]{0:T(1024)(128)(2,1)S(1)}, bf16[768]{0:T(1024)(128)(2,1)S(1)}, bf16[768]{0:T(1024)(128)(2,1)S(1)}, bf16[768]{0:T(1024)(128)(2,1)S(1)}...) all-reduce(bf16[768]{0:T(1024)(128)(2,1)S(1)} %dynamic-update-slice, ...), channel_id=1, replica_groups=mesh['shard'=4,'ctx'=8] {'shard'}, use_global_device_ids=true, to_apply=%add.7 | all-reduce | flops 9984 | bytes 39936
  611.3 15.0 %all-reduce.17 = (bf16[192]{0:T(256)(128)(2,1)S(1)}, bf16[192]{0:T(256)(128)(2,1)S(1)}, bf16[192]{0:T(256)(128)(2,1)S(1)}, bf16[192]{0:T(256)(128)(2,1)S(1)}, bf...) all-reduce(bf16[192]{0:T(256)(128)(2,1)S(1)} %dynamic-slice.9, ...), channel_id=1, replica_groups=mesh['shard'=4,'ctx'=8] {'ctx'}, use_global_device_ids=true, to_apply=%region_21.22 | all-reduce | flops 2304 | bytes 9216 | tf_op jit(solution)/shard_map/psum | solution.py:268
  632.2 4.1 fusion.57
  636.3 50.1 %all-reduce.23.cloned.1.call-done = (bf16[192,2304]{0,1:T(8,128)(2,1)}, bf16[192,768]{1,0:T(8,128)(2,1)}, bf16[192,3072]{1,0:T(8,128)(2,1)}, bf16[768,768]{1,0:T(8,128)(2,1)}) async-done(((bf16[192,2304]{0,1:T(8,128)(2,1)}, bf16[192,768]{1,0:T(8,128)(2,1)}, bf16[192,3072]{1,0:T(8,128)(2,1)}, bf16[768,768]{1,0:T(8,128)(2,1)}), (bf16[192,2304]{0,1:T(8,128)(2,1)}, bf16[192,768]{1,0:T(8,128)(2,1)}, ...) | async-done | bytes 3538960 | tf_op jit(solution)/shard_map/psum | solution.py:267
  686.4 3.0 convert_element_type.243
  (317 shorter events, 158.4 us)
Async XLA Ops:
  7.2 52.7 %all-gather.7.cloned.1.call-start = ((), (), s32[]{:S(2)}) async-start(), calls=%async_computation.6 | async-start | bytes 4423680 | tf_op jit(solution)/shard_map/all_gather | solution.py:86
  7.9 156.8 %all-gather.9.cloned.1.call-start = ((), (), s32[]{:S(2)}) async-start(), calls=%async_computation.7 | async-start | bytes 1769472 | tf_op jit(solution)/shard_map/all_gather | solution.py:127
  63.0 1.8 copy-start.12
  63.9 100.8 %all-gather.11.cloned.1.call-start = ((), (), s32[]{:S(2)}) async-start(), calls=%async_computation.8 | async-start | bytes 1769472 | tf_op jit(solution)/shard_map/all_gather | solution.py:126
  64.7 141.2 %all-gather.13.cloned.1.call-start = ((), (), s32[]{:S(2)}) async-start(), calls=%async_computation.9 | async-start | bytes 1474560 | tf_op jit(solution)/shard_map/all_gather | solution.py:89
  64.8 27.6 %collective-permute-start = (bf16[1,768,768]{2,1,0:T(8,128)(2,1)S(1)}, bf16[1,768,768]{2,1,0:T(8,128)(2,1)S(1)}, u32[]{:S(2)}, u32[]{:S(2)}) collective-permute-start(bf16[1,768,768]{2,1,0:T(8,128)(2,1)S(1)} %bitcast.169), channel_id=1, source_target_pairs={{0,8},{8,0},{16,24},{24,16},{1,9},{9,1},{17,25},{25,17},{2,10},{10... | collective-permute-start | bytes 3538952 | tf_op jit(solution)/shard_map/ppermute | solution.py:24
  92.6 4.1 copy-start.17
  94.5 65.0 %collective-permute-start.1 = (bf16[2,768,768]{2,1,0:T(8,128)(2,1)}, bf16[2,768,768]{2,1,0:T(8,128)(2,1)}, u32[]{:S(2)}, u32[]{:S(2)}) collective-permute-start(bf16[2,768,768]{2,1,0:T(8,128)(2,1)} %get-tuple-element.297), channel_id=1, source_target_pairs={{0,16},{8,24},{16,0},{24,8},{1,17},{9,25},{17,1},{25,9},{2,18},{10... | collective-permute-start | bytes 7077896 | tf_op jit(solution)/shard_map/ppermute | solution.py:24
  96.0 118.3 %all-gather.15.cloned.1.call-start = ((), (), s32[]{:S(2)}) async-start(), calls=%async_computation.10 | async-start | bytes 5898240 | tf_op jit(solution)/shard_map/all_gather | solution.py:93
  96.6 253.0 %reduce-scatter.19.cloned.1.call-start = ((), (), s32[]{:S(2)}) async-start(), calls=%async_computation.14 | async-start | bytes 1769472
  164.8 41.8 %copy-start.3 = (bf16[1,128,768]{2,1,0:T(8,128)(2,1)S(1)}, bf16[1,128,768]{2,1,0:T(8,128)(2,1)}, u32[]{:S(2)}) copy-start(bf16[1,128,768]{2,1,0:T(8,128)(2,1)} %param.20) | copy-start | bytes 589828
  205.9 14.4 %copy-start.8 = (bf16[12,64,128]{2,1,0:T(8,128)(2,1)}, bf16[12,64,128]{2,1,0:T(8,128)(2,1)S(1)}, u32[]{:S(2)}) copy-start(bf16[12,64,128]{2,1,0:T(8,128)(2,1)S(1)} %convert_element_type.205) | copy-start | bytes 589828
  206.5 13.7 %slice-start = ((s8[4718592]{0:T(1024)(128)(4,1)}), s8[524288]{0:T(1024)(128)(4,1)S(1)}, s32[]{:S(2)}) async-start(s8[4718592]{0:T(1024)(128)(4,1)} %bitcast.153), calls=%async_computation.18 | async-start | bytes 1048576
  214.3 6.0 slice-start.1
  221.7 5.1 slice-start.2
  221.9 4.9 slice-start.3
  226.8 1.9 copy-start.1
  315.2 69.9 %reduce-scatter.21.cloned.1.call-start = ((), (), s32[]{:S(2)}) async-start(), calls=%async_computation.15 | async-start | bytes 1769472
  317.8 122.6 %reduce-scatter.23.cloned.1.call-start = ((), (), s32[]{:S(2)}) async-start(), calls=%async_computation.16 | async-start | bytes 4423680
  318.3 70.7 %copy-start.6 = (bf16[12,64,128]{2,1,0:T(8,128)(2,1)}, bf16[12,64,128]{2,1,0:T(8,128)(2,1)S(1)}, u32[]{:S(2)}) copy-start(bf16[12,64,128]{2,1,0:T(8,128)(2,1)S(1)} %get-tuple-element.300) | copy-start | bytes 589828
  386.2 2.8 copy-start.4
  394.8 2.6 copy-start.2
  394.8 77.9 %reduce-scatter.13.cloned.1.call-start = ((), (), s32[]{:S(2)}) async-start(), calls=%async_computation.11 | async-start | bytes 1474560 | tf_op jit(solution)/shard_map/reduce_scatter | solution.py:235
  397.4 135.2 %reduce-scatter.15.cloned.1.call-start = ((), (), s32[]{:S(2)}) async-start(), calls=%async_computation.12 | async-start | bytes 5898240 | tf_op jit(solution)/shard_map/reduce_scatter | solution.py:247
  401.1 191.5 %reduce-scatter.17.cloned.1.call-start = ((), (), s32[]{:S(2)}) async-start(), calls=%async_computation.13 | async-start | bytes 5898240 | tf_op jit(solution)/shard_map/reduce_scatter | solution.py:253
  404.7 281.7 %all-reduce.23.cloned.1.call-start = ((), (), s32[]{:S(2)}) async-start(), calls=%async_computation.17 | async-start | bytes 7667712 | tf_op jit(solution)/shard_map/psum | solution.py:267
  592.5 2.3 copy-start.18
  592.6 2.6 copy-start.15
  592.6 39.7 %copy-start.5 = (bf16[768,128]{1,0:T(8,128)(2,1)S(1)}, bf16[768,128]{1,0:T(8,128)(2,1)}, u32[]{:S(2)}) copy-start(bf16[768,128]{1,0:T(8,128)(2,1)} %copy-done.4) | copy-start | bytes 589828
  592.6 39.7 %copy-start.7 = (bf16[12,64,128]{2,1,0:T(8,128)(2,1)S(1)}, bf16[12,64,128]{2,1,0:T(8,128)(2,1)}, u32[]{:S(2)}) copy-start(bf16[12,64,128]{2,1,0:T(8,128)(2,1)} %copy-done.6) | copy-start | bytes 589828
  686.4 3.0 copy-start.11
  689.5 1.7 copy-start.13
  (5 other events, 5.6 us)
Sparse Core Ops, SparseCore 0:
  9.8 49.9 all-gather.6
  64.1 27.0 all-gather.8
  93.3 25.7 all-gather.10
  120.9 34.6 all-gather.12
  157.3 56.9 all-gather.14
  315.3 34.2 reduce-scatter.18
  352.4 32.5 reduce-scatter.20
  394.9 45.4 reduce-scatter.22
  444.0 28.6 reduce-scatter.12
  475.5 56.9 reduce-scatter.14
  535.6 56.9 reduce-scatter.16
  595.6 90.7 all-reduce.22
